TPU v7x, 32 devices: a whole 2x2x4 slice. The times are simulated.
32 devices in a mesh: groups: 2 (over y), sess: 4 (over z), inner: 2 (over x), rep: 2 (over core).
Axes of the slice: x: 2, y: 2, z: 4, core: 2. Of those that a mesh axis runs over, the one named last changes fastest.
Arguments:
- thinker_rows: bfloat16 [4096, 3584], P(('groups', 'sess', 'rep'), 'inner'), parts along dimension 0, may hold values from -6 to 6
- row_session: int32 [4096, 1], P(('groups', 'sess', 'rep')), parts along dimension 0, may hold values from 0 to 31; in each aligned block of 256 rows (0 to 255, 256 to 511, ...) at most 12 rows name the same one
- speaker_of: int32 [64], P('groups'), parts along dimension 0, may hold values from 0 to 7
- prompt_slot: int32 [16], P('groups'), parts along dimension 0, may hold values from 0 to 7, each once
- prompt_cache: bfloat16 [16, 1024, 1024], P(('groups', 'sess'), ('inner', 'rep')), parts along dimension 0, may hold values from -64 to 64
- proj_weight: bfloat16 [3584, 896], P('inner'), may hold values from -0.09375 to 0.09375
- attn_gain: bfloat16 [896], replicated, may hold values from 0.5 to 1.5
- q_weight: bfloat16 [896, 1536], replicated, may hold values from -0.1875 to 0.1875
- k_weight: bfloat16 [896, 512], replicated, may hold values from -0.625 to 0.625
- v_weight: bfloat16 [896, 512], replicated, may hold values from -0.1875 to 0.1875
- o_weight: bfloat16 [1536, 896], replicated, may hold values from -0.15625 to 0.15625
Outputs:
- voice_states: bfloat16 [64, 96, 896], P(('groups', 'sess', 'inner', 'rep')), parts along dimension 0
There are 2 independent parts, one for each index of `groups`. A program takes and returns all parts, laid end to end along the dimension named above; an argument that names none is the same for every part. Nothing has to cross between parts.
Inputs may be any that keep to these rules, and one draw needn't show every extreme that they name: `row_session`: column 0 names the session of the row. Within each block of 256 rows (rows b * 256 to (b + 1) * 256 - 1, the rows of one index of sess+rep) no session is named by more than 12 rows, a bound that some block reaches; every session is named by some row. `prompt_slot`: each slot holds exactly one speaker's prompt.
All inputs are finite; a program needn't handle non-finite values.
Results may differ from a plain program's by a relative error of at most 0.0071.
Values may be sent and summed in bfloat16 or wider, within the bound.
No kernel may reach another device: no remote copies, remote signals or barrier semaphores. Data moves between devices by JAX's collectives and lax.ppermute only.
A program may use at most 128 MiB of HBM per device.

v0:
```python
import jax
import jax.numpy as jnp
from jax import lax
from jax.sharding import PartitionSpec as P

H = 12
KVH = 4
HD = 128
PROMPT = 1024
SLOTS = 96
EPSILON = 1e-06
ROPE_BASE = 1000000.0


def rms_scale(states, gain):
    widened = states.astype(jnp.float32)
    factor = lax.rsqrt(jnp.mean(widened * widened, axis=-1, keepdims=True) + EPSILON)
    return (widened * factor * gain.astype(jnp.float32)).astype(jnp.bfloat16)


def rope_tables(slot_total):
    half_width = HD // 2
    inverse = ROPE_BASE ** (-(jnp.arange(half_width, dtype=jnp.float32) * 2.0) / HD)
    angles = (PROMPT + jnp.arange(slot_total)).astype(jnp.float32)[:, None] * inverse[None, :]
    cosine = jnp.concatenate([jnp.cos(angles), jnp.cos(angles)], axis=1)[:, None, :]
    sine_table = jnp.concatenate([jnp.sin(angles), jnp.sin(angles)], axis=1)[:, None, :]
    return (cosine, sine_table)


def rotate(vectors, cosine, sine_table):
    half_width = vectors.shape[-1] // 2
    turned = jnp.concatenate([-vectors[..., half_width:], vectors[..., :half_width]], axis=-1)
    return vectors * cosine + turned * sine_table


def attend(states, lengths, prompts, attn_gain, q_weight, k_weight, v_weight, o_weight):
    session_total, slot_total, model_width = states.shape
    flat_rows = states.reshape(session_total * slot_total, model_width)
    normed = rms_scale(flat_rows, attn_gain)
    cosine, sine_table = rope_tables(slot_total)
    query = rotate(
        jnp.dot(normed, q_weight, preferred_element_type=jnp.float32).reshape(
            session_total, slot_total, H, HD
        ),
        cosine,
        sine_table,
    ).astype(jnp.bfloat16)
    own_keys = rotate(
        jnp.dot(normed, k_weight, preferred_element_type=jnp.float32).reshape(
            session_total, slot_total, KVH, HD
        ),
        cosine,
        sine_table,
    ).astype(jnp.bfloat16)
    own_values = (
        jnp.dot(normed, v_weight, preferred_element_type=jnp.float32)
        .reshape(session_total, slot_total, KVH, HD)
        .astype(jnp.bfloat16)
    )
    prompt_keys = prompts[:, :, : KVH * HD].reshape(session_total, PROMPT, KVH, HD)
    prompt_values = prompts[:, :, KVH * HD :].reshape(session_total, PROMPT, KVH, HD)
    all_keys = jnp.concatenate([prompt_keys, own_keys], axis=1)
    all_values = jnp.concatenate([prompt_values, own_values], axis=1)
    key_place = jnp.arange(PROMPT + slot_total) - PROMPT
    query_place = jnp.arange(slot_total)
    allowed = (key_place[None, None, :] < 0) | (
        key_place[None, None, :] <= query_place[None, :, None]
    ) & (key_place[None, None, :] < lengths[:, None, None])
    per_group = H // KVH
    outputs = []
    for kv_head in range(KVH):
        query_group = query[:, :, kv_head * per_group : (kv_head + 1) * per_group]
        scores = jnp.einsum(
            "cqhd,ckd->chqk",
            query_group,
            all_keys[:, :, kv_head],
            preferred_element_type=jnp.float32,
        ) * HD ** (-0.5)
        scores = jnp.where(allowed[:, None], scores, -1e30)
        highest = jnp.max(scores, axis=-1, keepdims=True)
        powers = jnp.exp(scores - highest)
        weights = (powers / jnp.sum(powers, axis=-1, keepdims=True)).astype(jnp.bfloat16)
        outputs.append(
            jnp.einsum(
                "chqk,ckd->cqhd",
                weights,
                all_values[:, :, kv_head],
                preferred_element_type=jnp.float32,
            )
        )
    attended = (
        jnp.concatenate(outputs, axis=2)
        .reshape(session_total * slot_total, H * HD)
        .astype(jnp.bfloat16)
    )
    return flat_rows.astype(jnp.float32) + jnp.dot(
        attended, o_weight, preferred_element_type=jnp.float32
    )


def body(
    thinker_rows,
    row_session,
    speaker_of,
    prompt_slot,
    prompt_cache,
    proj_weight,
    attn_gain,
    q_weight,
    k_weight,
    v_weight,
    o_weight,
):
    sess_count = lax.axis_size("sess")
    inner_count = lax.axis_size("inner")
    rep_count = lax.axis_size("rep")
    owner_count = sess_count * rep_count
    session_all = speaker_of.shape[0]
    per_device = session_all // (owner_count * inner_count)
    per_owner = per_device * inner_count
    slot_cap = SLOTS // owner_count
    inner_place = lax.axis_index("inner")
    shard_place = lax.axis_index("sess")
    row_owner = row_session[:, 0]
    device_of = row_owner // per_device
    target = (
        (device_of // (inner_count * rep_count) * rep_count + device_of % rep_count) * per_owner
        + device_of // rep_count % inner_count * per_device
        + row_owner % per_device
    )
    row_order = jnp.arange(row_owner.shape[0])
    earlier = jnp.sum(
        (
            (row_owner[:, None] == row_owner[None, :]) & (row_order[None, :] < row_order[:, None])
        ).astype(jnp.int32),
        axis=1,
    )
    slot_place = target * slot_cap + earlier
    counts = jnp.sum(
        (target[:, None] == jnp.arange(owner_count * per_owner)[None, :]).astype(jnp.int32), axis=0
    ).reshape(owner_count, per_owner)
    partial_sum = jnp.dot(thinker_rows, proj_weight, preferred_element_type=jnp.float32)
    own_columns = lax.psum_scatter(partial_sum, "inner", scatter_dimension=1, tiled=True).astype(
        jnp.bfloat16
    )
    buffer = (
        jnp.zeros((owner_count * per_owner * slot_cap, own_columns.shape[1]), own_columns.dtype)
        .at[slot_place]
        .set(own_columns)
    )
    arrived = lax.all_to_all(
        buffer.reshape(owner_count, per_owner * slot_cap, own_columns.shape[1]),
        ("sess", "rep"),
        split_axis=0,
        concat_axis=0,
        tiled=True,
    )
    counts_in = lax.all_to_all(counts, ("sess", "rep"), split_axis=0, concat_axis=0, tiled=True)
    arrived_rows = arrived.reshape(owner_count, per_owner, slot_cap, arrived.shape[2])
    regrouped = lax.all_to_all(arrived_rows, "inner", split_axis=1, concat_axis=3, tiled=True)
    projected = jnp.transpose(regrouped, (1, 0, 2, 3)).reshape(
        per_device, owner_count * slot_cap, regrouped.shape[3]
    )
    own_counts = lax.dynamic_slice_in_dim(counts_in, inner_place * per_device, per_device, 1)
    offsets = jnp.cumsum(own_counts, axis=0) - own_counts
    lengths = jnp.sum(own_counts, axis=0)
    within = jnp.arange(slot_cap)
    position = jnp.transpose(offsets)[:, :, None] + within[None, None, :]
    live_slot = within[None, None, :] < jnp.transpose(own_counts)[:, :, None]
    position = jnp.where(live_slot, position, SLOTS).reshape(per_device, owner_count * slot_cap)
    session_rows = jnp.broadcast_to(jnp.arange(per_device)[:, None], position.shape)
    compact = (
        jnp.zeros((per_device, SLOTS, projected.shape[2]), jnp.bfloat16)
        .at[session_rows, position]
        .set(projected, mode="drop")
    )
    shard_sessions = per_device * inner_count * rep_count
    wanted_speaker = lax.dynamic_slice_in_dim(
        speaker_of, shard_place * shard_sessions, shard_sessions
    )
    speaker_table = jnp.arange(prompt_slot.shape[0])
    wanted_slot = jnp.sum(
        jnp.where(wanted_speaker[:, None] == speaker_table[None, :], prompt_slot[None, :], 0),
        axis=1,
    )
    piece = lax.all_gather(prompt_cache, "sess", axis=0, tiled=True)
    matching = (wanted_slot[:, None] == jnp.arange(piece.shape[0])[None, :]).astype(jnp.bfloat16)
    chosen = jnp.einsum("sp,ptc->stc", matching, piece, preferred_element_type=jnp.float32)
    prompts = lax.all_to_all(
        chosen.astype(jnp.bfloat16), ("inner", "rep"), split_axis=0, concat_axis=1, tiled=True
    )
    summed = attend(compact, lengths, prompts, attn_gain, q_weight, k_weight, v_weight, o_weight)
    live_rows = (jnp.arange(SLOTS)[None, :] < lengths[:, None]).reshape(-1, 1)
    return (
        jnp.where(live_rows, summed, 0.0)
        .astype(jnp.bfloat16)
        .reshape(per_device, SLOTS, summed.shape[1])
    )


def solution(mesh):
    in_specs = (
        P(("groups", "sess", "rep"), "inner"),
        P(("groups", "sess", "rep"), None),
        P("groups"),
        P("groups"),
        P(("groups", "sess"), ("inner", "rep"), None),
        P("inner", None),
        P(),
        P(),
        P(),
        P(),
        P(),
    )
    out_specs = P(("groups", "sess", "inner", "rep"), None, None)
    return jax.shard_map(body, mesh=mesh, in_specs=in_specs, out_specs=out_specs, check_vma=False)
```

profile of v0, /device:TPU:0, one launch (start us, length us, event | category | flops | bytes accessed | tf_op | source)
XLA Modules:
  0.0 214.4 jit_solution(5181493876565836849)
XLA Ops:
  7.4 1.9 copy-done
  9.3 3.5 %fusion.175 = f32[256,896]{0,1:T(8,128)} fusion(bf16[256,1792]{1,0:T(8,128)(2,1)} %param.11, bf16[1792,896]{1,0:T(8,128)(2,1)S(1)} %copy-done), kind=kOutput, calls=%fused_computation.189 | convolution fusion | flops 822083584 | bytes 5046272 | tf_op jit(solution)/shard_map/dot_general | solution.py:142
  14.4 6.3 %all-to-all-start = ((s32[8,1,4]{2,1,0:T(1,128)}), s32[8,1,4]{2,1,0:T(1,128)S(1)}, u32[]{:S(2)}, u32[]{:S(2)}) async-start(s32[8,1,4]{2,1,0:T(1,128)} %bitcast.1), calls=%async_computation | async-start | bytes 8192 | tf_op jit(solution)/shard_map/all_to_all | solution.py:158
  20.7 4.9 %copy.90 = bf16[896,1536]{0,1:T(8,128)(2,1)} copy(bf16[896,1536]{1,0:T(8,128)(2,1)} %param.18) | data formatting | bytes 5505024 | tf_op args[7]
  27.7 1.3 copy.101
  29.3 5.2 %reduce-scatter.2.cloned.1.call-done = f32[256,448]{0,1:T(8,128)} async-done(((f32[256,896]{0,1:T(8,128)}), f32[256,448]{0,1:T(8,128)}) %reduce-scatter.2.cloned.1.call-update) | async-done | bytes 458768 | tf_op jit(solution)/shard_map/reduce_scatter | solution.py:143
  35.7 2.2 %scatter_custom_fusion = bf16[384,448]{1,0:T(8,128)(2,1)} fusion(s32[256]{0:T(256)S(1)} %bitcast.200, bf16[256,448]{1,0:T(8,128)(2,1)S(1)} %copy.75, bf16[]{:T(256)} %constant.95.clone.1), kind=kCustom, calls=%fused_computation.98 | custom fusion | bytes 344066 | tf_op jit(solution)/shard_map/scatter | solution.py:149
  38.0 4.6 %all-to-all-start.1 = ((bf16[8,48,448]{2,1,0:T(8,128)(2,1)}), bf16[8,48,448]{2,1,0:T(8,128)(2,1)S(1)}, u32[]{:S(2)}, u32[]{:S(2)}) async-start(bf16[8,48,448]{2,1,0:T(8,128)(2,1)} %bitcast.8), calls=%async_computation.2 | async-start | bytes 786432 | tf_op jit(solution)/shard_map/all_to_all | solution.py:151
  43.7 24.4 %all-to-all-done.1 = bf16[8,48,448]{2,1,0:T(8,128)(2,1)S(1)} async-done(((bf16[8,48,448]{2,1,0:T(8,128)(2,1)}), bf16[8,48,448]{2,1,0:T(8,128)(2,1)S(1)}, u32[]{:S(2)}, u32[]{:S(2)}) %all-to-all-start.1) | async-done | bytes 344096 | tf_op jit(solution)/shard_map/all_to_all | solution.py:151
  69.1 3.5 %all-to-all-start.2 = ((bf16[8,4,12,448]{3,0,2,1:T(8,128)(2,1)}), bf16[8,4,12,448]{3,0,2,1:T(8,128)(2,1)S(1)}, u32[]{:S(2)}, u32[]{:S(2)}) async-start(bf16[8,4,12,448]{3,0,2,1:T(8,128)(2,1)} %bitcast.9), calls=%async_computation.3 | async-start | bytes 786432 | tf_op jit(solution)/shard_map/all_to_all | solution.py:160
  72.5 33.9 %all-gather.2.cloned.1.call-done = bf16[8,256,1024]{2,1,0:T(8,128)(2,1)} async-done(((bf16[2,256,1024]{2,1,0:T(8,128)(2,1)}), bf16[8,256,1024]{2,1,0:T(8,128)(2,1)}) %all-gather.2.cloned.1.call-update) | async-done | bytes 4194320 | tf_op jit(solution)/shard_map/all_gather | solution.py:186
  106.4 4.7 %fusion.22 = bf16[8,256,1024]{2,0,1:T(8,128)(2,1)S(1)} fusion(bf16[8,256,1024]{2,1,0:T(8,128)(2,1)} %all-gather.2.cloned.1.call-done, s32[8]{0:T(128)S(1)} %select_reduce_fusion), kind=kOutput, calls=%fused_computation.34 | convolution fusion | flops 35651648 | bytes 8388640 | tf_op jit(solution)/shard_map/sp,ptc->stc/dot_general | solution.py:188
  111.2 4.3 %copy.80 = bf16[8,256,1024]{2,1,0:T(8,128)(2,1)} copy(bf16[8,256,1024]{2,0,1:T(8,128)(2,1)S(1)} %fusion.22) | data formatting | bytes 8388608 | tf_op jit(solution)/shard_map/convert_element_type | solution.py:190
  115.4 5.0 %all-to-all-start.3 = ((bf16[8,256,1024]{2,1,0:T(8,128)(2,1)}), bf16[8,256,1024]{2,1,0:T(8,128)(2,1)}, u32[]{:S(2)}, u32[]{:S(2)}) async-start(bf16[8,256,1024]{2,1,0:T(8,128)(2,1)} %copy.80), calls=%async_computation.4 | async-start | bytes 8388608 | tf_op jit(solution)/shard_map/all_to_all | solution.py:189
  122.3 13.1 %scatter_fusion = bf16[2,96,896]{2,1,0:T(8,128)(2,1)S(1)} fusion(bf16[2,96,896]{2,1,0:T(8,128)(2,1)S(1)} %broadcast_in_dim.55, s32[192]{0:T(256)S(1)} %reshape.305, bf16[192,896]{1,0:T(8,128)(2,1)S(1)} %reshape.307), kind=kCustom, calls=%fused_computation.1 | custom fusion | bytes 1033728 | tf_op jit(solution)/shard_map/scatter | solution.py:175
  137.1 1.2 convolution_convert_fusion
  138.3 1.1 fusion.113
  140.3 28.3 %all-to-all-done.3 = bf16[8,256,1024]{2,1,0:T(8,128)(2,1)} async-done(((bf16[8,256,1024]{2,1,0:T(8,128)(2,1)}), bf16[8,256,1024]{2,1,0:T(8,128)(2,1)}, u32[]{:S(2)}, u32[]{:S(2)}) %all-to-all-start.3) | async-done | bytes 4194336 | tf_op jit(solution)/shard_map/all_to_all | solution.py:189
  168.5 2.6 %copy.81 = bf16[2,4,256,1024]{3,2,1,0:T(8,128)(2,1)S(1)} copy(bf16[2,4,256,1024]{3,2,0,1:T(8,128)(2,1)} %bitcast.16) | data formatting | bytes 8388608 | tf_op jit(solution)/shard_map/all_to_all | solution.py:189
  171.1 2.5 %fusion.154 = (bf16[2,1024,512]{2,1,0:T(8,128)(2,1)}, bf16[2,1024,512]{2,1,0:T(8,128)(2,1)}) fusion(bf16[2,1024,1024]{2,1,0:T(8,128)(2,1)S(1)} %bitcast.185), kind=kLoop, calls=%fused_computation.184 | loop fusion | bytes 8388608 | tf_op jit(solution)/shard_map/slice | solution.py:61
  173.6 3.0 %copy.86 = bf16[2,1024,512]{1,2,0:T(8,128)(2,1)S(1)} copy(bf16[2,1024,512]{2,1,0:T(8,128)(2,1)} %get-tuple-element.10) | data formatting | bytes 4194304 | tf_op jit(solution)/shard_map/slice | solution.py:60
  176.7 2.5 %copy.88 = bf16[2,1024,4,128]{3,1,0,2:T(8,128)(2,1)} copy(bf16[2,1024,4,128]{1,3,2,0:T(8,128)(2,1)S(1)} %bitcast.187) | data formatting | bytes 4194304 | tf_op jit(solution)/shard_map/reshape | solution.py:60
  179.2 3.8 %fusion.155 = (f32[2,3,96]{2,1,0:T(4,128)S(1)}, f32[2,3,96,1120]{3,2,1,0:T(8,128)}) fusion(pred[2,96,1120]{2,1,0:T(8,128)(4,1)S(1)} %copy-done.9, bf16[2,1024,4,128]{3,1,0,2:T(8,128)(2,1)} %copy.88, bf16[2,96,12,128]{3,1,2,0:T(8,128)(2,1)S(1)} %fusion.32, bf16[2,96,4,128]{3,1,2,0:T(8,128)(2,1)S(1)} %copy-done.10), kind=kOutput, calls=%fused_computation.185 | convolution fusion | flops 168879200 | bytes 5245184 | tf_op jit(solution)/shard_map/sub | solution.py:81
  183.0 2.6 %fusion.160 = (f32[2,3,96]{2,1,0:T(4,128)S(1)}, f32[2,3,96,1120]{3,2,1,0:T(8,128)}) fusion(pred[2,96,1120]{2,1,0:T(8,128)(4,1)S(1)} %copy-done.9, bf16[2,1024,4,128]{3,1,0,2:T(8,128)(2,1)S(1)} %copy-done.4, bf16[2,96,12,128]{3,1,2,0:T(8,128)(2,1)S(1)} %fusion.32, bf16[2,96,4,128]{3,1,2,0:T(8,128)(2,1)S(1)} %copy-done.10), kind=kOutput, calls=%fused_computation.186 | convolution fusion | flops 168879200 | bytes 5245184 | tf_op jit(solution)/shard_map/sub | solution.py:81
  185.7 2.6 %fusion.165 = (f32[2,3,96]{2,1,0:T(4,128)S(1)}, f32[2,3,96,1120]{3,2,1,0:T(8,128)}) fusion(pred[2,96,1120]{2,1,0:T(8,128)(4,1)S(1)} %copy-done.9, bf16[2,1024,4,128]{3,1,0,2:T(8,128)(2,1)S(1)} %copy-done.4, bf16[2,96,12,128]{3,1,2,0:T(8,128)(2,1)S(1)} %fusion.32, bf16[2,96,4,128]{3,1,2,0:T(8,128)(2,1)S(1)} %copy-done.10), kind=kOutput, calls=%fused_computation.187 | convolution fusion | flops 168879200 | bytes 5245184 | tf_op jit(solution)/shard_map/sub | solution.py:81
  188.3 2.7 %fusion.170 = (f32[2,3,96]{2,1,0:T(4,128)S(1)}, f32[2,3,96,1120]{3,2,1,0:T(8,128)}) fusion(pred[2,96,1120]{2,1,0:T(8,128)(4,1)S(1)} %copy-done.9, bf16[2,1024,4,128]{3,1,0,2:T(8,128)(2,1)S(1)} %copy-done.4, bf16[2,96,12,128]{3,1,2,0:T(8,128)(2,1)S(1)} %fusion.32, bf16[2,96,4,128]{3,1,2,0:T(8,128)(2,1)S(1)} %copy-done.10), kind=kOutput, calls=%fused_computation.188 | convolution fusion | flops 168879200 | bytes 5245184 | tf_op jit(solution)/shard_map/sub | solution.py:81
  190.9 3.0 %copy.82 = bf16[2,1024,512]{1,2,0:T(8,128)(2,1)S(1)} copy(bf16[2,1024,512]{2,1,0:T(8,128)(2,1)} %get-tuple-element.9) | data formatting | bytes 4194304 | tf_op jit(solution)/shard_map/slice | solution.py:61
  193.9 2.9 %copy.84 = bf16[2,1024,4,128]{3,1,0,2:T(8,128)(2,1)} copy(bf16[2,1024,4,128]{1,3,2,0:T(8,128)(2,1)S(1)} %bitcast.188) | data formatting | bytes 4194304 | tf_op jit(solution)/shard_map/reshape | solution.py:61
  196.8 2.6 %fusion.40 = bf16[2,96,3,128]{3,1,2,0:T(8,128)(2,1)S(1)} fusion(f32[2,3,96,1120]{3,2,1,0:T(8,128)} %get-tuple-element.18, f32[2,3,96]{2,1,0:T(4,128)S(1)} %get-tuple-element.17, bf16[2,1024,4,128]{3,1,0,2:T(8,128)(2,1)} %copy.84, bf16[2,96,4,128]{3,1,2,0:T(8,128)(2,1)S(1)} %copy-done.17), kind=kOutput, calls=%fused_computation.64 | convolution fusion | flops 167661568 | bytes 5024000 | tf_op jit(solution)/shard_map/chqk,ckd->cqhd/dot_general | solution.py:84
  200.7 1.2 copy-done.19
  202.5 1.2 copy-done.18
  205.4 1.5 fusion.30
  (96 shorter events, 15.2 us)
Async XLA Ops:
  7.4 1.9 copy-start
  7.4 6.0 %copy-start.11 = (s32[256,1]{0,1:T(1,128)S(1)}, s32[256,1]{0,1:T(1,128)}, u32[]{:S(2)}) copy-start(s32[256,1]{0,1:T(1,128)} %param.12) | copy-start | bytes 3076
  7.4 27.1 %reduce-scatter.2.cloned.1.call-start = ((), (), s32[]{:S(2)}) async-start(), calls=%async_computation.5 | async-start | bytes 1376256 | tf_op jit(solution)/shard_map/reduce_scatter | solution.py:143
  12.8 93.7 %all-gather.2.cloned.1.call-start = ((), (), s32[]{:S(2)}) async-start(), calls=%async_computation.6 | async-start | bytes 5242880 | tf_op jit(solution)/shard_map/all_gather | solution.py:186
  14.4 14.6 %all-to-all-start = ((s32[8,1,4]{2,1,0:T(1,128)}), s32[8,1,4]{2,1,0:T(1,128)S(1)}, u32[]{:S(2)}, u32[]{:S(2)}) async-start(s32[8,1,4]{2,1,0:T(1,128)} %bitcast.1), calls=%async_computation | async-start | bytes 8192 | tf_op jit(solution)/shard_map/all_to_all | solution.py:158
  20.7 5.0 %copy-start.12 = (bf16[896]{0:T(1024)(128)(2,1)S(1)}, bf16[896]{0:T(1024)(128)(2,1)}, u32[]{:S(2)}) copy-start(bf16[896]{0:T(1024)(128)(2,1)} %param.17) | copy-start | bytes 5380
  20.7 5.0 %copy-start.5 = (bf16[896,512]{1,0:T(8,128)(2,1)S(1)}, bf16[896,512]{1,0:T(8,128)(2,1)}, u32[]{:S(2)}) copy-start(bf16[896,512]{1,0:T(8,128)(2,1)} %param.19) | copy-start | bytes 2752516
  20.7 5.6 %copy-start.14 = (s32[32]{0:T(128)S(1)}, s32[32]{0:T(128)}, u32[]{:S(2)}) copy-start(s32[32]{0:T(128)} %param.13) | copy-start | bytes 388
  20.7 5.7 %copy-start.15 = (s32[8]{0:T(128)S(1)}, s32[8]{0:T(128)}, u32[]{:S(2)}) copy-start(s32[8]{0:T(128)} %param.14) | copy-start | bytes 100
  25.6 2.1 copy-start.6
  38.0 30.1 %all-to-all-start.1 = ((bf16[8,48,448]{2,1,0:T(8,128)(2,1)}), bf16[8,48,448]{2,1,0:T(8,128)(2,1)S(1)}, u32[]{:S(2)}, u32[]{:S(2)}) async-start(bf16[8,48,448]{2,1,0:T(8,128)(2,1)} %bitcast.8), calls=%async_computation.2 | async-start | bytes 786432 | tf_op jit(solution)/shard_map/all_to_all | solution.py:151
  69.1 46.4 %all-to-all-start.2 = ((bf16[8,4,12,448]{3,0,2,1:T(8,128)(2,1)}), bf16[8,4,12,448]{3,0,2,1:T(8,128)(2,1)S(1)}, u32[]{:S(2)}, u32[]{:S(2)}) async-start(bf16[8,4,12,448]{3,0,2,1:T(8,128)(2,1)} %bitcast.9), calls=%async_computation.3 | async-start | bytes 786432 | tf_op jit(solution)/shard_map/all_to_all | solution.py:160
  115.4 53.1 %all-to-all-start.3 = ((bf16[8,256,1024]{2,1,0:T(8,128)(2,1)}), bf16[8,256,1024]{2,1,0:T(8,128)(2,1)}, u32[]{:S(2)}, u32[]{:S(2)}) async-start(bf16[8,256,1024]{2,1,0:T(8,128)(2,1)} %copy.80), calls=%async_computation.4 | async-start | bytes 8388608 | tf_op jit(solution)/shard_map/all_to_all | solution.py:189
  135.3 0.9 copy-start.8
  135.5 1.6 copy-start.7
  136.0 2.2 %copy-start.2 = (bf16[896,1536]{0,1:T(8,128)(2,1)S(1)}, bf16[896,1536]{0,1:T(8,128)(2,1)}, u32[]{:S(2)}) copy-start(bf16[896,1536]{0,1:T(8,128)(2,1)} %copy.90) | copy-start | bytes 8257540
  176.6 2.6 %copy-start.9 = (pred[2,96,1120]{2,1,0:T(8,128)(4,1)S(1)}, pred[2,96,1120]{2,1,0:T(8,128)(4,1)}, u32[]{:S(2)}) copy-start(pred[2,96,1120]{2,1,0:T(8,128)(4,1)} %and_or_fusion) | copy-start | bytes 645124
  176.6 2.6 %copy-start.10 = (bf16[2,96,4,128]{3,1,2,0:T(8,128)(2,1)S(1)}, bf16[2,96,4,128]{3,1,2,0:T(8,128)(2,1)}, u32[]{:S(2)}) copy-start(bf16[2,96,4,128]{3,1,2,0:T(8,128)(2,1)} %fusion.68) | copy-start | bytes 589828
  179.2 3.8 %copy-start.4 = (bf16[2,1024,4,128]{3,1,0,2:T(8,128)(2,1)S(1)}, bf16[2,1024,4,128]{3,1,0,2:T(8,128)(2,1)}, u32[]{:S(2)}) copy-start(bf16[2,1024,4,128]{3,1,0,2:T(8,128)(2,1)} %copy.88) | copy-start | bytes 6291460
  193.9 2.9 %copy-start.17 = (bf16[2,96,4,128]{3,1,2,0:T(8,128)(2,1)S(1)}, bf16[2,96,4,128]{3,1,2,0:T(8,128)(2,1)}, u32[]{:S(2)}) copy-start(bf16[2,96,4,128]{3,1,2,0:T(8,128)(2,1)} %convolution_convert_fusion) | copy-start | bytes 589828
  196.8 2.6 %copy-start.3 = (bf16[2,1024,4,128]{3,1,0,2:T(8,128)(2,1)S(1)}, bf16[2,1024,4,128]{3,1,0,2:T(8,128)(2,1)}, u32[]{:S(2)}) copy-start(bf16[2,1024,4,128]{3,1,0,2:T(8,128)(2,1)} %copy.84) | copy-start | bytes 6291460
  196.8 3.3 %copy-start.20 = (f32[2,3,96,1120]{3,2,1,0:T(8,128)S(1)}, f32[2,3,96,1120]{3,2,1,0:T(8,128)}, u32[]{:S(2)}) copy-start(f32[2,3,96,1120]{3,2,1,0:T(8,128)} %get-tuple-element.20) | copy-start | bytes 7741444
  200.1 1.7 copy-start.19
  201.9 1.7 copy-start.18
  203.6 1.8 copy-start.13
  204.2 1.2 copy-start.16
  204.6 2.4 %copy-start.1 = (bf16[1792,896]{1,0:T(8,128)(2,1)S(1)}, bf16[1792,896]{1,0:T(8,128)(2,1)}, u32[]{:S(2)}) copy-start(bf16[1792,896]{1,0:T(8,128)(2,1)} %param.16) | copy-start | bytes 9633796
Sparse Core Ops, SparseCore 0:
  12.9 21.5 reduce-scatter.1
Sparse Core Ops, SparseCore 1:
  14.8 91.6 all-gather.1
where the time goes:
time: 215 us; the launch traced here: 214 us
  waiting for transfers between devices  92.3 us (43%)
  local copies, waits for them, and re-layouts  52.8 us (25%)
  matrix products  28.5 us (13%)
  starting transfers between devices  19.5 us (9%)
  between operations  15.2 us (7%)
  other arithmetic  6.03 us (3%)
    all_gather x1, waiting for transfers between devices, body(): piece = lax.all_gather(prompt_cache, 'sess', axis=0, tiled=True)  33.9 us
    all_to_all x1, waiting for transfers between devices, body(): lax.all_to_all(chosen.astype(jnp.bfloat16), ('inner', 'rep'), split_axis=...  28.3 us
    all_to_all x1, waiting for transfers between devices, body(): lax.all_to_all(buffer.reshape(owner_count, per_owner * slot_cap, own_colu...  24.4 us
    scatter x1, local copies, waits for them, and re-layouts, body(): compact = jnp.zeros((per_device, SLOTS, projected.shape[2]), jnp.bfloat16...  13.1 us
    sub x4, matrix products, attend(): powers = jnp.exp(scores - highest)  11.7 us
    unnamed x43, local copies, waits for them, and re-layouts  10.7 us
    all_to_all x1, starting transfers between devices, body(): lax.all_to_all(counts, ('sess', 'rep'), split_axis=0, concat_axis=0, tile...  6.33 us
    slice x2, local copies, waits for them, and re-layouts, attend(): prompts[:, :, KVH * HD:].reshape(session_total, PROMPT, KVH, HD)  5.48 us
  transfers between devices with their start and end apart: 6, of which 4 were waited for; matrix products, arithmetic and copies ran while one was open for 20% of the time, Pallas kernels for 0%

commit v1 on v0

--- a/solution.py
+++ b/solution.py
@@ -148,13 +148,20 @@
         .at[slot_place]
         .set(own_columns)
     )
-    arrived = lax.all_to_all(
-        buffer.reshape(owner_count, per_owner * slot_cap, own_columns.shape[1]),
-        ("sess", "rep"),
-        split_axis=0,
-        concat_axis=0,
-        tiled=True,
-    )
+    x = buffer.reshape(owner_count, per_owner * slot_cap, own_columns.shape[1])
+    ways, here = (lax.axis_size(("sess", "rep")), lax.axis_index(("sess", "rep")))
+    width = x.shape[0] // ways
+    shape = list(x.shape)
+    shape[0] = width
+    height = shape[0]
+    shape[0] = height * ways
+    full = jnp.zeros(shape, x.dtype)
+    for mask in range(ways):
+        part = lax.dynamic_slice_in_dim(x, (here ^ mask) * width, width, axis=0)
+        if mask:
+            part = lax.ppermute(part, ("sess", "rep"), [(d, d ^ mask) for d in range(ways)])
+        full = lax.dynamic_update_slice_in_dim(full, part, (here ^ mask) * height, axis=0)
+    arrived = full
     counts_in = lax.all_to_all(counts, ("sess", "rep"), split_axis=0, concat_axis=0, tiled=True)
     arrived_rows = arrived.reshape(owner_count, per_owner, slot_cap, arrived.shape[2])
     regrouped = lax.all_to_all(arrived_rows, "inner", split_axis=1, concat_axis=3, tiled=True)

time: 215 us -> 224 us (1.042)
  local copies, waits for them, and re-layouts: 52.8 us -> 77.1 us
  waiting for transfers between devices: 92.3 us -> 70.2 us
  starting transfers between devices: 19.5 us -> 25.4 us
    all_to_all x1 -> x0, waiting for transfers between devices: 24.4 us -> none  [body(): lax.all_to_all(buffer.reshape(owner_count, per_owner * slot_cap, own_colu...]
    dynamic_update_slice x0 -> x8, local copies, waits for them, and re-layouts: none -> 24 us  [body(): lax.dynamic_update_slice_in_dim(full, part, (here ^ mask) * height, axis=0)]
    ppermute x0 -> x7, starting transfers between devices: none -> 10.3 us  [body(): lax.ppermute(part, ('sess', 'rep'), [(d, d ^ mask) for d in range(ways)])]
    ppermute x0 -> x7, waiting for transfers between devices: none -> 6.69 us  [body(): lax.ppermute(part, ('sess', 'rep'), [(d, d ^ mask) for d in range(ways)])]
    all_to_all x1 -> x0, starting transfers between devices: 4.63 us -> none  [body(): lax.all_to_all(buffer.reshape(owner_count, per_owner * slot_cap, own_colu...]
    all_gather x1, waiting for transfers between devices: 33.9 us -> 30.4 us  [body(): piece = lax.all_gather(prompt_cache, 'sess', axis=0, tiled=True)]
    unnamed x43 -> x51, local copies, waits for them, and re-layouts: 10.7 us -> 11.8 us
  transfers between devices with their start and end apart: 6 -> 12, of which waited for: 4 -> 4; matrix products, arithmetic and copies ran while one was open for 20% -> 30% of each run, Pallas kernels for 0% -> 0%
where the time goes in v1:
time: 224 us; the launch traced here: 223 us
  local copies, waits for them, and re-layouts  77.1 us (34%)
  waiting for transfers between devices  70.2 us (31%)
  matrix products  28.5 us (13%)
  starting transfers between devices  25.4 us (11%)
  between operations  15.3 us (7%)
  other arithmetic  6.03 us (3%)
    all_gather x1, waiting for transfers between devices, body(): piece = lax.all_gather(prompt_cache, 'sess', axis=0, tiled=True)  30.4 us
    all_to_all x1, waiting for transfers between devices, body(): lax.all_to_all(chosen.astype(jnp.bfloat16), ('inner', 'rep'), split_axis=...  28.2 us
    dynamic_update_slice x8, local copies, waits for them, and re-layouts, body(): lax.dynamic_update_slice_in_dim(full, part, (here ^ mask) * height, axis=0)  24 us
    scatter x1, local copies, waits for them, and re-layouts, body(): compact = jnp.zeros((per_device, SLOTS, projected.shape[2]), jnp.bfloat16...  13.1 us
    unnamed x51, local copies, waits for them, and re-layouts  11.8 us
    sub x4, matrix products, attend(): powers = jnp.exp(scores - highest)  11.7 us
    ppermute x7, starting transfers between devices, body(): lax.ppermute(part, ('sess', 'rep'), [(d, d ^ mask) for d in range(ways)])  10.3 us
    ppermute x7, waiting for transfers between devices, body(): lax.ppermute(part, ('sess', 'rep'), [(d, d ^ mask) for d in range(ways)])  6.69 us
  transfers between devices with their start and end apart: 12, of which 4 were waited for; matrix products, arithmetic and copies ran while one was open for 30% of the time, Pallas kernels for 0%

profile of v1, /device:TPU:0, one launch (start us, length us, event | category | flops | bytes accessed | tf_op | source)
XLA Modules:
  0.0 222.6 jit_solution(16809155013802886784)
XLA Ops:
  9.3 3.4 %fusion.175 = f32[256,896]{0,1:T(8,128)} fusion(bf16[256,1792]{1,0:T(8,128)(2,1)} %param.11, bf16[1792,896]{1,0:T(8,128)(2,1)S(1)} %copy-done), kind=kOutput, calls=%fused_computation.197 | convolution fusion | flops 822083584 | bytes 5046272 | tf_op jit(solution)/shard_map/dot_general | solution.py:142
  14.4 6.3 %all-to-all-start = ((s32[8,1,4]{2,1,0:T(1,128)}), s32[8,1,4]{2,1,0:T(1,128)S(1)}, u32[]{:S(2)}, u32[]{:S(2)}) async-start(s32[8,1,4]{2,1,0:T(1,128)} %bitcast.1), calls=%async_computation | async-start | bytes 8192 | tf_op jit(solution)/shard_map/all_to_all | solution.py:165
  20.7 4.8 %copy.118 = bf16[896,1536]{0,1:T(8,128)(2,1)} copy(bf16[896,1536]{1,0:T(8,128)(2,1)} %param.18) | data formatting | bytes 5505024 | tf_op args[7]
  30.1 4.4 %reduce-scatter.2.cloned.1.call-done = f32[256,448]{0,1:T(8,128)} async-done(((f32[256,896]{0,1:T(8,128)}), f32[256,448]{0,1:T(8,128)}) %reduce-scatter.2.cloned.1.call-update) | async-done | bytes 458768 | tf_op jit(solution)/shard_map/reduce_scatter | solution.py:143
  39.8 2.5 %collective-permute-start.3 = (bf16[1,48,448]{2,0,1:T(2,128)(2,1)S(1)}, bf16[1,48,448]{2,0,1:T(2,128)(2,1)S(1)}, u32[]{:S(2)}, u32[]{:S(2)}) collective-permute-start(bf16[1,48,448]{2,0,1:T(2,128)(2,1)S(1)} %copy.135), channel_id=1, source_target_pairs={{0,8},{1,9},{4,12},{5,13},{8,0},{9,1},{12,4},{13,5},{2,10},{3,11},... | collective-permute-start | bytes 129032 | tf_op jit(solution)/shard_map/ppermute | solution.py:162
  42.7 3.4 %collective-permute-start.5 = (bf16[1,48,448]{2,0,1:T(2,128)(2,1)S(1)}, bf16[1,48,448]{2,0,1:T(2,128)(2,1)S(1)}, u32[]{:S(2)}, u32[]{:S(2)}) collective-permute-start(bf16[1,48,448]{2,0,1:T(2,128)(2,1)S(1)} %copy.137), channel_id=1, source_target_pairs={{0,12},{1,13},{4,8},{5,9},{8,4},{9,5},{12,0},{13,1},{2,14},{3,15},... | collective-permute-start | bytes 129032 | tf_op jit(solution)/shard_map/ppermute | solution.py:162
  46.1 6.7 %collective-permute-done.1 = bf16[1,48,448]{2,0,1:T(2,128)(2,1)S(1)} collective-permute-done((bf16[1,48,448]{2,0,1:T(2,128)(2,1)S(1)}, bf16[1,48,448]{2,0,1:T(2,128)(2,1)S(1)}, u32[]{:S(2)}, u32[]{:S(2)}) %collective-permute-start.1) | collective-permute-done | bytes 43040 | tf_op jit(solution)/shard_map/ppermute | solution.py:162
  56.7 3.0 %dynamic_update_slice.24 = bf16[8,48,448]{2,0,1:T(8,128)(2,1)} dynamic-update-slice(bf16[8,48,448]{2,0,1:T(8,128)(2,1)} %broadcast_in_dim.60, bf16[1,48,448]{2,0,1:T(2,128)(2,1)S(1)} %copy.131, s32[]{:T(128)S(6)} %select_n.135, s32[]{:T(128)} %constant.97.clone.1, s32[]{:T(128)} %constant.97.clone.1) | dynamic-update-slice | bytes 86020 | tf_op jit(solution)/shard_map/dynamic_update_slice | solution.py:163
  59.7 3.0 %dynamic_update_slice.25 = bf16[8,48,448]{2,0,1:T(8,128)(2,1)} dynamic-update-slice(bf16[8,48,448]{2,0,1:T(8,128)(2,1)} %dynamic_update_slice.24, bf16[1,48,448]{2,0,1:T(2,128)(2,1)S(1)} %collective-permute-done, s32[]{:T(128)S(6)} %select_n.136, s32[]{:T(128)} %constant.97.clone.1, s32[]{:T(128)} %constant.97.clone.1) | dynamic-update-slice | bytes 86020 | tf_op jit(solution)/shard_map/dynamic_update_slice | solution.py:163
  62.7 3.0 %dynamic_update_slice.26 = bf16[8,48,448]{2,0,1:T(8,128)(2,1)} dynamic-update-slice(bf16[8,48,448]{2,0,1:T(8,128)(2,1)} %dynamic_update_slice.25, bf16[1,48,448]{2,0,1:T(2,128)(2,1)S(1)} %collective-permute-done.1, s32[]{:T(128)S(6)} %select_n.137, s32[]{:T(128)} %constant.97.clone.1, s32[]{:T(128)} %constant.97.clone.1) | dynamic-update-slice | bytes 86020 | tf_op jit(solution)/shard_map/dynamic_update_slice | solution.py:163
  65.7 3.0 %dynamic_update_slice.27 = bf16[8,48,448]{2,0,1:T(8,128)(2,1)} dynamic-update-slice(bf16[8,48,448]{2,0,1:T(8,128)(2,1)} %dynamic_update_slice.26, bf16[1,48,448]{2,0,1:T(2,128)(2,1)S(1)} %collective-permute-done.2, s32[]{:T(128)S(6)} %select_n.138, s32[]{:T(128)} %constant.97.clone.1, s32[]{:T(128)} %constant.97.clone.1) | dynamic-update-slice | bytes 86020 | tf_op jit(solution)/shard_map/dynamic_update_slice | solution.py:163
  68.7 3.0 %dynamic_update_slice.28 = bf16[8,48,448]{2,0,1:T(8,128)(2,1)} dynamic-update-slice(bf16[8,48,448]{2,0,1:T(8,128)(2,1)} %dynamic_update_slice.27, bf16[1,48,448]{2,0,1:T(2,128)(2,1)S(1)} %collective-permute-done.3, s32[]{:T(128)S(6)} %select_n.139, s32[]{:T(128)} %constant.97.clone.1, s32[]{:T(128)} %constant.97.clone.1) | dynamic-update-slice | bytes 86020 | tf_op jit(solution)/shard_map/dynamic_update_slice | solution.py:163
  71.7 3.0 %dynamic_update_slice.29 = bf16[8,48,448]{2,0,1:T(8,128)(2,1)} dynamic-update-slice(bf16[8,48,448]{2,0,1:T(8,128)(2,1)} %dynamic_update_slice.28, bf16[1,48,448]{2,0,1:T(2,128)(2,1)S(1)} %collective-permute-done.4, s32[]{:T(128)S(6)} %select_n.140, s32[]{:T(128)} %constant.97.clone.1, s32[]{:T(128)} %constant.97.clone.1) | dynamic-update-slice | bytes 86020 | tf_op jit(solution)/shard_map/dynamic_update_slice | solution.py:163
  74.7 3.0 %dynamic_update_slice.30 = bf16[8,48,448]{2,0,1:T(8,128)(2,1)} dynamic-update-slice(bf16[8,48,448]{2,0,1:T(8,128)(2,1)} %dynamic_update_slice.29, bf16[1,48,448]{2,0,1:T(2,128)(2,1)S(1)} %collective-permute-done.5, s32[]{:T(128)S(6)} %select_n.141, s32[]{:T(128)} %constant.97.clone.1, s32[]{:T(128)} %constant.97.clone.1) | dynamic-update-slice | bytes 86020 | tf_op jit(solution)/shard_map/dynamic_update_slice | solution.py:163
  77.7 3.0 %dynamic_update_slice.31 = bf16[8,48,448]{2,0,1:T(8,128)(2,1)} dynamic-update-slice(bf16[8,48,448]{2,0,1:T(8,128)(2,1)} %dynamic_update_slice.30, bf16[1,48,448]{2,0,1:T(2,128)(2,1)S(1)} %collective-permute-done.6, s32[]{:T(128)S(6)} %select_n.142, s32[]{:T(128)} %constant.97.clone.1, s32[]{:T(128)} %constant.97.clone.1) | dynamic-update-slice | bytes 86020 | tf_op jit(solution)/shard_map/dynamic_update_slice | solution.py:163
  80.6 3.6 %all-to-all-start.1 = ((bf16[8,4,12,448]{3,0,2,1:T(8,128)(2,1)}), bf16[8,4,12,448]{3,0,2,1:T(8,128)(2,1)S(1)}, u32[]{:S(2)}, u32[]{:S(2)}) async-start(bf16[8,4,12,448]{3,0,2,1:T(8,128)(2,1)} %bitcast.9), calls=%async_computation.2 | async-start | bytes 786432 | tf_op jit(solution)/shard_map/all_to_all | solution.py:167
  84.3 30.4 %all-gather.2.cloned.1.call-done = bf16[8,256,1024]{2,1,0:T(8,128)(2,1)} async-done(((bf16[2,256,1024]{2,1,0:T(8,128)(2,1)}), bf16[8,256,1024]{2,1,0:T(8,128)(2,1)}) %all-gather.2.cloned.1.call-update) | async-done | bytes 4194320 | tf_op jit(solution)/shard_map/all_gather | solution.py:193
  114.7 4.7 %fusion.22 = bf16[8,256,1024]{2,0,1:T(8,128)(2,1)S(1)} fusion(bf16[8,256,1024]{2,1,0:T(8,128)(2,1)} %all-gather.2.cloned.1.call-done, s32[8]{0:T(128)S(1)} %select_reduce_fusion), kind=kOutput, calls=%fused_computation.34 | convolution fusion | flops 35651648 | bytes 8388640 | tf_op jit(solution)/shard_map/sp,ptc->stc/dot_general | solution.py:195
  119.4 4.3 %copy.108 = bf16[8,256,1024]{2,1,0:T(8,128)(2,1)} copy(bf16[8,256,1024]{2,0,1:T(8,128)(2,1)S(1)} %fusion.22) | data formatting | bytes 8388608 | tf_op jit(solution)/shard_map/convert_element_type | solution.py:197
  123.7 5.1 %all-to-all-start.2 = ((bf16[8,256,1024]{2,1,0:T(8,128)(2,1)}), bf16[8,256,1024]{2,1,0:T(8,128)(2,1)}, u32[]{:S(2)}, u32[]{:S(2)}) async-start(bf16[8,256,1024]{2,1,0:T(8,128)(2,1)} %copy.108), calls=%async_computation.3 | async-start | bytes 8388608 | tf_op jit(solution)/shard_map/all_to_all | solution.py:196
  130.6 13.1 %scatter_fusion = bf16[2,96,896]{2,1,0:T(8,128)(2,1)S(1)} fusion(bf16[2,96,896]{2,1,0:T(8,128)(2,1)S(1)} %broadcast_in_dim.57, s32[192]{0:T(256)S(1)} %reshape.305, bf16[192,896]{1,0:T(8,128)(2,1)S(1)} %reshape.307), kind=kCustom, calls=%fused_computation.1 | custom fusion | bytes 1033728 | tf_op jit(solution)/shard_map/scatter | solution.py:182
  148.6 28.2 %all-to-all-done.2 = bf16[8,256,1024]{2,1,0:T(8,128)(2,1)} async-done(((bf16[8,256,1024]{2,1,0:T(8,128)(2,1)}), bf16[8,256,1024]{2,1,0:T(8,128)(2,1)}, u32[]{:S(2)}, u32[]{:S(2)}) %all-to-all-start.2) | async-done | bytes 4194336 | tf_op jit(solution)/shard_map/all_to_all | solution.py:196
  176.8 2.6 %copy.109 = bf16[2,4,256,1024]{3,2,1,0:T(8,128)(2,1)S(1)} copy(bf16[2,4,256,1024]{3,2,0,1:T(8,128)(2,1)} %bitcast.16) | data formatting | bytes 8388608 | tf_op jit(solution)/shard_map/all_to_all | solution.py:196
  181.8 3.0 %copy.114 = bf16[2,1024,512]{1,2,0:T(8,128)(2,1)S(1)} copy(bf16[2,1024,512]{2,1,0:T(8,128)(2,1)} %get-tuple-element.10) | data formatting | bytes 4194304 | tf_op jit(solution)/shard_map/slice | solution.py:60
  184.9 2.6 %copy.116 = bf16[2,1024,4,128]{3,1,0,2:T(8,128)(2,1)} copy(bf16[2,1024,4,128]{1,3,2,0:T(8,128)(2,1)S(1)} %bitcast.187) | data formatting | bytes 4194304 | tf_op jit(solution)/shard_map/reshape | solution.py:60
  187.5 3.8 %fusion.155 = (f32[2,3,96]{2,1,0:T(4,128)S(1)}, f32[2,3,96,1120]{3,2,1,0:T(8,128)}) fusion(pred[2,96,1120]{2,1,0:T(8,128)(4,1)S(1)} %copy-done.9, bf16[2,1024,4,128]{3,1,0,2:T(8,128)(2,1)} %copy.116, bf16[2,96,12,128]{3,1,2,0:T(8,128)(2,1)S(1)} %fusion.32, bf16[2,96,4,128]{3,1,2,0:T(8,128)(2,1)S(1)} %copy-done.10), kind=kOutput, calls=%fused_computation.193 | convolution fusion | flops 168879200 | bytes 5245184 | tf_op jit(solution)/shard_map/sub | solution.py:81
  191.3 2.6 %fusion.160 = (f32[2,3,96]{2,1,0:T(4,128)S(1)}, f32[2,3,96,1120]{3,2,1,0:T(8,128)}) fusion(pred[2,96,1120]{2,1,0:T(8,128)(4,1)S(1)} %copy-done.9, bf16[2,1024,4,128]{3,1,0,2:T(8,128)(2,1)S(1)} %copy-done.4, bf16[2,96,12,128]{3,1,2,0:T(8,128)(2,1)S(1)} %fusion.32, bf16[2,96,4,128]{3,1,2,0:T(8,128)(2,1)S(1)} %copy-done.10), kind=kOutput, calls=%fused_computation.194 | convolution fusion | flops 168879200 | bytes 5245184 | tf_op jit(solution)/shard_map/sub | solution.py:81
  193.9 2.6 %fusion.165 = (f32[2,3,96]{2,1,0:T(4,128)S(1)}, f32[2,3,96,1120]{3,2,1,0:T(8,128)}) fusion(pred[2,96,1120]{2,1,0:T(8,128)(4,1)S(1)} %copy-done.9, bf16[2,1024,4,128]{3,1,0,2:T(8,128)(2,1)S(1)} %copy-done.4, bf16[2,96,12,128]{3,1,2,0:T(8,128)(2,1)S(1)} %fusion.32, bf16[2,96,4,128]{3,1,2,0:T(8,128)(2,1)S(1)} %copy-done.10), kind=kOutput, calls=%fused_computation.195 | convolution fusion | flops 168879200 | bytes 5245184 | tf_op jit(solution)/shard_map/sub | solution.py:81
  196.5 2.7 %fusion.170 = (f32[2,3,96]{2,1,0:T(4,128)S(1)}, f32[2,3,96,1120]{3,2,1,0:T(8,128)}) fusion(pred[2,96,1120]{2,1,0:T(8,128)(4,1)S(1)} %copy-done.9, bf16[2,1024,4,128]{3,1,0,2:T(8,128)(2,1)S(1)} %copy-done.4, bf16[2,96,12,128]{3,1,2,0:T(8,128)(2,1)S(1)} %fusion.32, bf16[2,96,4,128]{3,1,2,0:T(8,128)(2,1)S(1)} %copy-done.10), kind=kOutput, calls=%fused_computation.196 | convolution fusion | flops 168879200 | bytes 5245184 | tf_op jit(solution)/shard_map/sub | solution.py:81
  199.2 3.0 %copy.110 = bf16[2,1024,512]{1,2,0:T(8,128)(2,1)S(1)} copy(bf16[2,1024,512]{2,1,0:T(8,128)(2,1)} %get-tuple-element.9) | data formatting | bytes 4194304 | tf_op jit(solution)/shard_map/slice | solution.py:61
  202.2 2.8 %copy.112 = bf16[2,1024,4,128]{3,1,0,2:T(8,128)(2,1)} copy(bf16[2,1024,4,128]{1,3,2,0:T(8,128)(2,1)S(1)} %bitcast.188) | data formatting | bytes 4194304 | tf_op jit(solution)/shard_map/reshape | solution.py:61
  205.0 2.6 %fusion.40 = bf16[2,96,3,128]{3,1,2,0:T(8,128)(2,1)S(1)} fusion(f32[2,3,96,1120]{3,2,1,0:T(8,128)} %get-tuple-element.26, f32[2,3,96]{2,1,0:T(4,128)S(1)} %get-tuple-element.25, bf16[2,1024,4,128]{3,1,0,2:T(8,128)(2,1)} %copy.112, bf16[2,96,4,128]{3,1,2,0:T(8,128)(2,1)S(1)} %copy-done.17), kind=kOutput, calls=%fused_computation.64 | convolution fusion | flops 167661568 | bytes 5024000 | tf_op jit(solution)/shard_map/chqk,ckd->cqhd/dot_general | solution.py:84
  (125 shorter events, 34.0 us)
Async XLA Ops:
  7.4 1.9 copy-start
  7.4 6.0 %copy-start.11 = (s32[256,1]{0,1:T(1,128)S(1)}, s32[256,1]{0,1:T(1,128)}, u32[]{:S(2)}) copy-start(s32[256,1]{0,1:T(1,128)} %param.12) | copy-start | bytes 3076
  7.4 27.1 %reduce-scatter.2.cloned.1.call-start = ((), (), s32[]{:S(2)}) async-start(), calls=%async_computation.4 | async-start | bytes 1376256 | tf_op jit(solution)/shard_map/reduce_scatter | solution.py:143
  12.7 101.9 %all-gather.2.cloned.1.call-start = ((), (), s32[]{:S(2)}) async-start(), calls=%async_computation.5 | async-start | bytes 5242880 | tf_op jit(solution)/shard_map/all_gather | solution.py:193
  14.4 15.0 %all-to-all-start = ((s32[8,1,4]{2,1,0:T(1,128)}), s32[8,1,4]{2,1,0:T(1,128)S(1)}, u32[]{:S(2)}, u32[]{:S(2)}) async-start(s32[8,1,4]{2,1,0:T(1,128)} %bitcast.1), calls=%async_computation | async-start | bytes 8192 | tf_op jit(solution)/shard_map/all_to_all | solution.py:165
  20.7 4.9 %copy-start.12 = (bf16[896]{0:T(1024)(128)(2,1)S(1)}, bf16[896]{0:T(1024)(128)(2,1)}, u32[]{:S(2)}) copy-start(bf16[896]{0:T(1024)(128)(2,1)} %param.17) | copy-start | bytes 5380
  20.7 4.9 %copy-start.5 = (bf16[896,512]{1,0:T(8,128)(2,1)S(1)}, bf16[896,512]{1,0:T(8,128)(2,1)}, u32[]{:S(2)}) copy-start(bf16[896,512]{1,0:T(8,128)(2,1)} %param.19) | copy-start | bytes 2752516
  25.5 1.2 copy-start.6
  25.5 2.5 %copy-start.14 = (s32[32]{0:T(128)S(1)}, s32[32]{0:T(128)}, u32[]{:S(2)}) copy-start(s32[32]{0:T(128)} %param.13) | copy-start | bytes 388
  25.5 2.6 %copy-start.15 = (s32[8]{0:T(128)S(1)}, s32[8]{0:T(128)}, u32[]{:S(2)}) copy-start(s32[8]{0:T(128)} %param.14) | copy-start | bytes 100
  37.5 5.2 %collective-permute-start = (bf16[1,48,448]{2,0,1:T(2,128)(2,1)S(1)}, bf16[1,48,448]{2,0,1:T(2,128)(2,1)S(1)}, u32[]{:S(2)}, u32[]{:S(2)}) collective-permute-start(bf16[1,48,448]{2,0,1:T(2,128)(2,1)S(1)} %copy.132), channel_id=1, source_target_pairs={{0,1},{1,0},{4,5},{5,4},{8,9},{9,8},{12,13},{13,12},{2,3},{3,2},{6... | collective-permute-start | bytes 129032 | tf_op jit(solution)/shard_map/ppermute | solution.py:162
  37.6 15.2 %collective-permute-start.1 = (bf16[1,48,448]{2,0,1:T(2,128)(2,1)S(1)}, bf16[1,48,448]{2,0,1:T(2,128)(2,1)S(1)}, u32[]{:S(2)}, u32[]{:S(2)}) collective-permute-start(bf16[1,48,448]{2,0,1:T(2,128)(2,1)S(1)} %copy.133), channel_id=1, source_target_pairs={{0,4},{1,5},{4,0},{5,1},{8,12},{9,13},{12,8},{13,9},{2,6},{3,7},{6... | collective-permute-start | bytes 129032 | tf_op jit(solution)/shard_map/ppermute | solution.py:162
  39.3 26.4 %collective-permute-start.2 = (bf16[1,48,448]{2,0,1:T(2,128)(2,1)S(1)}, bf16[1,48,448]{2,0,1:T(2,128)(2,1)S(1)}, u32[]{:S(2)}, u32[]{:S(2)}) collective-permute-start(bf16[1,48,448]{2,0,1:T(2,128)(2,1)S(1)} %copy.134), channel_id=1, source_target_pairs={{0,5},{1,4},{4,1},{5,0},{8,13},{9,12},{12,9},{13,8},{2,7},{3,6},{6... | collective-permute-start | bytes 129032 | tf_op jit(solution)/shard_map/ppermute | solution.py:162
  39.8 28.9 %collective-permute-start.3 = (bf16[1,48,448]{2,0,1:T(2,128)(2,1)S(1)}, bf16[1,48,448]{2,0,1:T(2,128)(2,1)S(1)}, u32[]{:S(2)}, u32[]{:S(2)}) collective-permute-start(bf16[1,48,448]{2,0,1:T(2,128)(2,1)S(1)} %copy.135), channel_id=1, source_target_pairs={{0,8},{1,9},{4,12},{5,13},{8,0},{9,1},{12,4},{13,5},{2,10},{3,11},... | collective-permute-start | bytes 129032 | tf_op jit(solution)/shard_map/ppermute | solution.py:162
  42.3 29.3 %collective-permute-start.4 = (bf16[1,48,448]{2,0,1:T(2,128)(2,1)S(1)}, bf16[1,48,448]{2,0,1:T(2,128)(2,1)S(1)}, u32[]{:S(2)}, u32[]{:S(2)}) collective-permute-start(bf16[1,48,448]{2,0,1:T(2,128)(2,1)S(1)} %copy.136), channel_id=1, source_target_pairs={{0,9},{1,8},{4,13},{5,12},{8,1},{9,0},{12,5},{13,4},{2,11},{3,10},... | collective-permute-start | bytes 129032 | tf_op jit(solution)/shard_map/ppermute | solution.py:162
  42.7 31.9 %collective-permute-start.5 = (bf16[1,48,448]{2,0,1:T(2,128)(2,1)S(1)}, bf16[1,48,448]{2,0,1:T(2,128)(2,1)S(1)}, u32[]{:S(2)}, u32[]{:S(2)}) collective-permute-start(bf16[1,48,448]{2,0,1:T(2,128)(2,1)S(1)} %copy.137), channel_id=1, source_target_pairs={{0,12},{1,13},{4,8},{5,9},{8,4},{9,5},{12,0},{13,1},{2,14},{3,15},... | collective-permute-start | bytes 129032 | tf_op jit(solution)/shard_map/ppermute | solution.py:162
  52.8 24.9 %collective-permute-start.6 = (bf16[1,48,448]{2,0,1:T(2,128)(2,1)S(1)}, bf16[1,48,448]{2,0,1:T(2,128)(2,1)S(1)}, u32[]{:S(2)}, u32[]{:S(2)}) collective-permute-start(bf16[1,48,448]{2,0,1:T(2,128)(2,1)S(1)} %copy.138), channel_id=1, source_target_pairs={{0,13},{1,12},{4,9},{5,8},{8,5},{9,4},{12,1},{13,0},{2,15},{3,14},... | collective-permute-start | bytes 129032 | tf_op jit(solution)/shard_map/ppermute | solution.py:162
  80.6 43.0 %all-to-all-start.1 = ((bf16[8,4,12,448]{3,0,2,1:T(8,128)(2,1)}), bf16[8,4,12,448]{3,0,2,1:T(8,128)(2,1)S(1)}, u32[]{:S(2)}, u32[]{:S(2)}) async-start(bf16[8,4,12,448]{3,0,2,1:T(8,128)(2,1)} %bitcast.9), calls=%async_computation.2 | async-start | bytes 786432 | tf_op jit(solution)/shard_map/all_to_all | solution.py:167
  123.7 53.1 %all-to-all-start.2 = ((bf16[8,256,1024]{2,1,0:T(8,128)(2,1)}), bf16[8,256,1024]{2,1,0:T(8,128)(2,1)}, u32[]{:S(2)}, u32[]{:S(2)}) async-start(bf16[8,256,1024]{2,1,0:T(8,128)(2,1)} %copy.108), calls=%async_computation.3 | async-start | bytes 8388608 | tf_op jit(solution)/shard_map/all_to_all | solution.py:196
  143.8 1.6 copy-start.7
  144.3 2.2 %copy-start.2 = (bf16[896,1536]{0,1:T(8,128)(2,1)S(1)}, bf16[896,1536]{0,1:T(8,128)(2,1)}, u32[]{:S(2)}) copy-start(bf16[896,1536]{0,1:T(8,128)(2,1)} %copy.118) | copy-start | bytes 8257540
  184.8 2.6 %copy-start.9 = (pred[2,96,1120]{2,1,0:T(8,128)(4,1)S(1)}, pred[2,96,1120]{2,1,0:T(8,128)(4,1)}, u32[]{:S(2)}) copy-start(pred[2,96,1120]{2,1,0:T(8,128)(4,1)} %and_or_fusion) | copy-start | bytes 645124
  184.9 2.6 %copy-start.10 = (bf16[2,96,4,128]{3,1,2,0:T(8,128)(2,1)S(1)}, bf16[2,96,4,128]{3,1,2,0:T(8,128)(2,1)}, u32[]{:S(2)}) copy-start(bf16[2,96,4,128]{3,1,2,0:T(8,128)(2,1)} %fusion.68) | copy-start | bytes 589828
  187.5 3.8 %copy-start.4 = (bf16[2,1024,4,128]{3,1,0,2:T(8,128)(2,1)S(1)}, bf16[2,1024,4,128]{3,1,0,2:T(8,128)(2,1)}, u32[]{:S(2)}) copy-start(bf16[2,1024,4,128]{3,1,0,2:T(8,128)(2,1)} %copy.116) | copy-start | bytes 6291460
  202.2 2.9 %copy-start.17 = (bf16[2,96,4,128]{3,1,2,0:T(8,128)(2,1)S(1)}, bf16[2,96,4,128]{3,1,2,0:T(8,128)(2,1)}, u32[]{:S(2)}) copy-start(bf16[2,96,4,128]{3,1,2,0:T(8,128)(2,1)} %convolution_convert_fusion) | copy-start | bytes 589828
  205.0 2.6 %copy-start.3 = (bf16[2,1024,4,128]{3,1,0,2:T(8,128)(2,1)S(1)}, bf16[2,1024,4,128]{3,1,0,2:T(8,128)(2,1)}, u32[]{:S(2)}) copy-start(bf16[2,1024,4,128]{3,1,0,2:T(8,128)(2,1)} %copy.112) | copy-start | bytes 6291460
  205.0 3.3 %copy-start.20 = (f32[2,3,96,1120]{3,2,1,0:T(8,128)S(1)}, f32[2,3,96,1120]{3,2,1,0:T(8,128)}, u32[]{:S(2)}) copy-start(f32[2,3,96,1120]{3,2,1,0:T(8,128)} %get-tuple-element.28) | copy-start | bytes 7741444
  208.4 1.7 copy-start.19
  210.1 1.7 copy-start.18
  211.9 1.8 copy-start.13
  212.5 1.2 copy-start.16
  212.8 2.4 %copy-start.1 = (bf16[1792,896]{1,0:T(8,128)(2,1)S(1)}, bf16[1792,896]{1,0:T(8,128)(2,1)}, u32[]{:S(2)}) copy-start(bf16[1792,896]{1,0:T(8,128)(2,1)} %param.16) | copy-start | bytes 9633796
  (1 other events, 0.9 us)
Sparse Core Ops, SparseCore 0:
  12.9 21.5 reduce-scatter.1
Sparse Core Ops, SparseCore 1:
  14.8 99.8 all-gather.1
